TPU v7x, 256 devices: a whole 4x4x8 slice. The times are simulated.
256 devices in a mesh: ep: 32 (over z, y), tp: 8 (over x, core).
Axes of the slice: x: 4, y: 4, z: 8, core: 2. Of those that a mesh axis runs over, the one named last changes fastest.
Arguments:
- tokens: bfloat16 [4096, 2048], P('ep', 'tp'), may hold values from -200 to 200
- norm_gain: bfloat16 [2048], P('tp'), may hold values from 0.099609375 to 1.8984375
- router_logits: float32 [4096, 64], P('ep'), may hold values from -8 to 400
- routes: int32 [4096, 8], P('ep'), may hold values from 0 to 63, all different within a row; in each aligned block of 128 rows (0 to 127, 128 to 255, ...) at most 32 rows name the same one
- gate_proj: bfloat16 [64, 2048, 1024], P('ep', None, 'tp'), may hold values from -0.125 to 0.125
- up_proj: bfloat16 [64, 2048, 1024], P('ep', None, 'tp'), may hold values from -0.125 to 0.125
- down_proj: bfloat16 [64, 1024, 2048], P('ep', 'tp'), may hold values from -0.1875 to 0.1875
Outputs:
- mixed: bfloat16 [4096, 2048], P('ep', 'tp')
Inputs may be any that keep to these rules, and one draw needn't show every extreme that they name: `routes`: within each aligned block of 128 rows (the tokens of one index of ep) no expert is named by more than 32 rows, a bound that some block reaches; a row names 8 different experts.
All inputs are finite; a program needn't handle non-finite values.
Results may differ from a plain program's by a relative error of at most 0.0071.
Values may be sent and summed in bfloat16 or wider, within the bound.
No kernel may reach another device: no remote copies, remote signals or barrier semaphores. Data moves between devices by JAX's collectives and lax.ppermute only.
A program may use at most 128 MiB of HBM per device.

v0:
```python
import jax
import jax.numpy as jnp
from jax import lax
from jax.sharding import PartitionSpec as P

epsilon = 1e-05


def on_device(tokens, norm_gain, router_logits, routes, gate_proj, up_proj, down_proj):
    ep_count = lax.axis_size("ep")
    group_size = tokens.shape[0]
    width = tokens.shape[1]
    top_count = routes.shape[1]
    local_experts = gate_proj.shape[0]
    expert_count = local_experts * ep_count
    capacity = 2 * group_size * top_count // expert_count
    slot_count = expert_count * capacity
    expert_iota = jnp.arange(expert_count, dtype=jnp.int32)
    flat_routes = routes.reshape(-1)
    route_hits = (flat_routes[:, None] == expert_iota[None, :]).astype(jnp.int32)
    position = jnp.sum((jnp.cumsum(route_hits, axis=0) - route_hits) * route_hits, axis=1)
    slot_grid = (flat_routes * capacity + position).reshape(group_size, top_count)
    chosen = jnp.sum(
        jnp.where(routes[:, :, None] == expert_iota[None, None, :], router_logits[:, None, :], 0.0),
        axis=-1,
    )
    gates = jax.nn.softmax(chosen, axis=-1)
    matches = jnp.arange(slot_count, dtype=jnp.int32)[:, None, None] == slot_grid[None, :, :]
    dispatch_table = jnp.any(matches, axis=-1).astype(jnp.bfloat16)
    whole, gain_all = (
        lax.all_gather(tokens, "tp", axis=1, tiled=True),
        lax.all_gather(norm_gain, "tp", axis=0, tiled=True),
    )
    floated = whole.astype(jnp.float32)
    mean_square = jnp.mean(floated * floated, axis=-1, keepdims=True)
    normed = (floated * lax.rsqrt(mean_square + epsilon) * gain_all.astype(jnp.float32)).astype(
        jnp.bfloat16
    )
    outgoing = jnp.dot(dispatch_table, normed, preferred_element_type=jnp.float32).astype(
        jnp.bfloat16
    )
    arrived = lax.all_to_all(outgoing, "ep", split_axis=0, concat_axis=0, tiled=True)
    arrived = arrived.reshape(ep_count, local_experts, capacity, arrived.shape[1])
    gate_val = jnp.einsum("slcd,ldh->slch", arrived, gate_proj, preferred_element_type=jnp.float32)
    up_val = jnp.einsum("slcd,ldh->slch", arrived, up_proj, preferred_element_type=jnp.float32)
    hidden = (jax.nn.silu(gate_val) * up_val).astype(jnp.bfloat16)
    term = jnp.einsum("slch,lhd->dslc", hidden, down_proj, preferred_element_type=jnp.float32)
    summed = lax.psum_scatter(
        term.reshape(width * lax.axis_size("tp"), slot_count), "tp", scatter_dimension=0, tiled=True
    )
    returned = lax.all_to_all(
        summed.astype(jnp.bfloat16), "ep", split_axis=1, concat_axis=1, tiled=True
    )
    slot_rows = jnp.transpose(returned)
    picked = slot_rows[slot_grid].astype(jnp.float32)
    mixed = jnp.sum(gates[:, :, None] * picked, axis=1)
    return mixed.astype(jnp.bfloat16)


def solution(mesh):
    return jax.shard_map(
        on_device,
        mesh=mesh,
        in_specs=(
            P("ep", "tp"),
            P("tp"),
            P("ep", None),
            P("ep", None),
            P("ep", None, "tp"),
            P("ep", None, "tp"),
            P("ep", "tp", None),
        ),
        out_specs=P("ep", "tp"),
        check_vma=False,
    )
```

profile of v0, /device:TPU:8, one launch (start us, length us, event | category | flops | bytes accessed | tf_op | source)
XLA Modules:
  0.0 431.7 jit_solution(2664050021449953185)
XLA Ops:
  6.5 0.9 copy.44
  7.4 0.1 eq.59
  7.5 0.1 eq.55
  7.6 18.0 %reduce-window.6 = s32[64,8,128]{2,1,0:T(8,128)S(1)} reduce-window(s32[64,8,128]{2,1,0:T(8,128)S(1)} %fusion.39, s32[]{:T(128)} %constant.12.clone.1), window={size=1x1x128 pad=0_0x0_0x127_0}, to_apply=%region_3.4 | reduce-window | flops 8323072 | bytes 524292 | tf_op jit(solution)/shard_map/reduce-window
  25.6 0.1 slice.10
  25.8 0.1 copy.46
  26.0 0.1 copy.47
  26.0 0.1 broadcast_add_fusion
  26.2 0.1 fusion.38
  26.3 0.1 reduce_sum.50
  26.4 0.7 compare_select_fusion
  27.1 7.4 %fusion = pred[2048,128]{1,0:T(8,128)(4,1)S(1)} fusion(s32[128,8]{0,1:T(8,128)S(1)} %get-tuple-element.6), kind=kLoop, calls=%fused_computation.2 | loop fusion | flops 3932160 | bytes 266240 | tf_op jit(solution)/shard_map/reduce_or | solution.py:29
  34.5 13.7 %all_gather.6 = bf16[128,2048]{1,0:T(8,128)(2,1)S(1)} all-gather(bf16[128,256]{1,0:T(8,128)(2,1)} %param.7), channel_id=1, replica_groups=mesh['ep'=32,'tp'=8] {'tp'}, dimensions={1}, use_global_device_ids=true | all-gather | bytes 589824 | tf_op jit(solution)/shard_map/all_gather | solution.py:31
  48.2 0.2 fusion.19
  48.4 0.7 reshape.97
  49.1 10.2 %all-gather = bf16[8,1,256]{2,1,0:T(2,128)(2,1)S(1)} all-gather(bf16[1,1,256]{2,1,0:T(2,128)(2,1)S(1)} %reshape.97), channel_id=1, replica_groups=mesh['ep'=32,'tp'=8] {'tp'}, dimensions={0}, use_global_device_ids=true | all-gather | bytes 4608 | tf_op jit(solution)/shard_map/all_gather | solution.py:32
  59.3 2.4 convolution_convert_fusion
  61.7 197.5 %all_to_all.21 = bf16[32,64,2048]{2,1,0:T(8,128)(2,1)S(1)} all-to-all(bf16[32,64,2048]{2,1,0:T(8,128)(2,1)S(1)} %bitcast.59), channel_id=1, replica_groups=mesh['ep'=32,'tp'=8] {'ep'}, dimensions={0} | all-to-all | bytes 16777216 | tf_op jit(solution)/shard_map/all_to_all | solution.py:42
  259.2 3.2 copy-done.1
  262.4 2.3 fusion.5
  264.7 14.1 %convolution_bitcast_fusion = f32[2048,32,2,32]{0,3,1,2:T(8,128)} fusion(bf16[32,2,32,2048]{3,2,1,0:T(8,128)(2,1)} %bitcast.61, bf16[2,128,2048]{2,1,0:T(8,128)(2,1)S(1)} %copy-done, bf16[2,2048,128]{2,1,0:T(8,128)(2,1)S(1)} %copy-done.2, f32[32,2,32,128]{3,2,0,1:T(8,128)S(1)} %fusion.5), kind=kOutput, calls=%fused_computation.8 | convolution fusion | flops 2149056512 | bytes 28311552 | tf_op jit(solution)/shard_map/slch,lhd->dslc/dot_general | solution.py:47
  278.9 11.6 %copy.51 = f32[2048,32,2,32]{0,3,2,1:T(8,128)} copy(f32[2048,32,2,32]{0,3,1,2:T(8,128)} %convolution_bitcast_fusion) | data formatting | bytes 33554432 | tf_op jit(solution)/shard_map/slch,lhd->dslc/transpose | solution.py:47
  290.5 0.0 reduce-scatter.2.cloned.1.call-update
  290.5 89.0 %reduce-scatter.2.cloned.1.call-done = f32[256,2048]{0,1:T(8,128)} async-done(((f32[2048,2048]{0,1:T(8,128)}), f32[256,2048]{0,1:T(8,128)}) %reduce-scatter.2.cloned.1.call-update) | async-done | bytes 2097168 | tf_op jit(solution)/shard_map/reduce_scatter | solution.py:48
  379.5 2.7 convert_element_type.39
  382.2 10.2 %all-to-all-start.1 = ((bf16[256,32,64]{0,2,1:T(8,128)(2,1)}), bf16[256,32,64]{0,2,1:T(8,128)(2,1)S(1)}, u32[]{:S(2)}, u32[]{:S(2)}) async-start(bf16[256,32,64]{0,2,1:T(8,128)(2,1)} %bitcast.15), calls=%async_computation.2 | async-start | bytes 2097152 | tf_op jit(solution)/shard_map/all_to_all | solution.py:51
  392.4 0.1 copy.52
  392.5 0.1 reshape.88
  392.7 0.1 copy.43
  392.8 27.1 %all-to-all-done.1 = bf16[256,32,64]{0,2,1:T(8,128)(2,1)S(1)} async-done(((bf16[256,32,64]{0,2,1:T(8,128)(2,1)}), bf16[256,32,64]{0,2,1:T(8,128)(2,1)S(1)}, u32[]{:S(2)}, u32[]{:S(2)}) %all-to-all-start.1) | async-done | bytes 1048608 | tf_op jit(solution)/shard_map/all_to_all | solution.py:51
  419.9 3.9 gather_fusion
  423.8 1.0 fusion.22
  (23 shorter events, 0.2 us)
Async XLA Ops:
  6.5 258.2 %copy-start = (bf16[2,128,2048]{2,1,0:T(8,128)(2,1)S(1)}, bf16[2,128,2048]{2,1,0:T(8,128)(2,1)}, u32[]{:S(2)}) copy-start(bf16[2,128,2048]{2,1,0:T(8,128)(2,1)} %param.13) | copy-start | bytes 3145732
  6.5 373.0 %reduce-scatter.2.cloned.1.call-start = ((), (), s32[]{:S(2)}) async-start(), calls=%async_computation.3 | async-start | bytes 18874368 | tf_op jit(solution)/shard_map/reduce_scatter | solution.py:48
  61.7 200.7 %copy-start.5 = (bf16[2,2048,128]{2,1,0:T(8,128)(2,1)S(1)}, bf16[2,2048,128]{2,1,0:T(8,128)(2,1)}, u32[]{:S(2)}) copy-start(bf16[2,2048,128]{2,1,0:T(8,128)(2,1)} %param.11) | copy-start | bytes 3145732
  259.2 3.2 copy-start.1
  259.2 5.6 %copy-start.2 = (bf16[2,2048,128]{2,1,0:T(8,128)(2,1)S(1)}, bf16[2,2048,128]{2,1,0:T(8,128)(2,1)}, u32[]{:S(2)}) copy-start(bf16[2,2048,128]{2,1,0:T(8,128)(2,1)} %param.12) | copy-start | bytes 3145732
  290.5 102.1 %copy-start.3 = (s32[128,8]{0,1:T(8,128)S(1)}, s32[128,8]{0,1:T(8,128)}, u32[]{:S(2)}) copy-start(s32[128,8]{0,1:T(8,128)} %param.10) | copy-start | bytes 12292
  290.5 102.1 %copy-start.4 = (f32[128,64]{0,1:T(8,128)S(1)}, f32[128,64]{0,1:T(8,128)}, u32[]{:S(2)}) copy-start(f32[128,64]{0,1:T(8,128)} %param.9) | copy-start | bytes 98308
  382.2 37.7 %all-to-all-start.1 = ((bf16[256,32,64]{0,2,1:T(8,128)(2,1)}), bf16[256,32,64]{0,2,1:T(8,128)(2,1)S(1)}, u32[]{:S(2)}, u32[]{:S(2)}) async-start(bf16[256,32,64]{0,2,1:T(8,128)(2,1)} %bitcast.15), calls=%async_computation.2 | async-start | bytes 2097152 | tf_op jit(solution)/shard_map/all_to_all | solution.py:51
Sparse Core Ops, SparseCore 0:
  290.6 88.8 reduce-scatter.1
where the time goes:
time: 432 us
  blocking collectives  221 us (51%)
  waiting for transfers between devices  116 us (27%)
  other arithmetic  30.4 us (7%)
  local copies, waits for them, and re-layouts  21.3 us (5%)
  matrix products  18.8 us (4%)
  between operations  13.6 us (3%)
  starting transfers between devices  10.2 us (2%)
    all_to_all x1, blocking collectives, on_device(): lax.all_to_all(outgoing, 'ep', split_axis=0, concat_axis=0, tiled=True)  197 us
    reduce_scatter x1, waiting for transfers between devices, on_device(): lax.psum_scatter(term.reshape(width * lax.axis_size('tp'), slot_count), '...  89 us
    all_to_all x1, waiting for transfers between devices, on_device(): lax.all_to_all(summed.astype(jnp.bfloat16), 'ep', split_axis=1, concat_ax...  27.1 us
    another operation x3, other arithmetic  18.2 us
    dot_general x1, matrix products, on_device(): jnp.einsum('slch,lhd->dslc', hidden, down_proj, preferred_element_type=jn...  14.1 us
    all_gather x1, blocking collectives, on_device(): lax.all_gather(tokens, 'tp', axis=1, tiled=True)  13.7 us
    transpose x1, local copies, waits for them, and re-layouts, on_device(): jnp.einsum('slch,lhd->dslc', hidden, down_proj, preferred_element_type=jn...  11.6 us
    all_gather x1, blocking collectives, on_device(): lax.all_gather(norm_gain, 'tp', axis=0, tiled=True)  10.2 us
  transfers between devices with their start and end apart: 2, of which 2 were waited for; matrix products, arithmetic and copies ran while one was open for 0% of the time, Pallas kernels for 0%

commit v1 on v0

--- a/solution.py
+++ b/solution.py
@@ -48,8 +48,14 @@
     summed = lax.psum_scatter(
         term.reshape(width * lax.axis_size("tp"), slot_count), "tp", scatter_dimension=0, tiled=True
     )
-    returned = lax.all_to_all(
-        summed.astype(jnp.bfloat16), "ep", split_axis=1, concat_axis=1, tiled=True
+    returned = jnp.concatenate(
+        lax.all_to_all(
+            jnp.stack(jnp.split(summed.astype(jnp.bfloat16), lax.axis_size("ep"), axis=1)),
+            "ep",
+            0,
+            0,
+        ),
+        axis=1,
     )
     slot_rows = jnp.transpose(returned)
     picked = slot_rows[slot_grid].astype(jnp.float32)

time: 432 us -> 450 us (1.042)
  local copies, waits for them, and re-layouts: 21.3 us -> 40.7 us
    unnamed x14 -> x45, local copies, waits for them, and re-layouts: 4.78 us -> 23.5 us
where the time goes in v1:
time: 450 us
  blocking collectives  221 us (49%)
  waiting for transfers between devices  116 us (26%)
  local copies, waits for them, and re-layouts  40.7 us (9%)
  other arithmetic  29.4 us (7%)
  matrix products  18.8 us (4%)
  between operations  13.6 us (3%)
  starting transfers between devices  10.2 us (2%)
    all_to_all x1, blocking collectives, on_device(): lax.all_to_all(outgoing, 'ep', split_axis=0, concat_axis=0, tiled=True)  197 us
    reduce_scatter x1, waiting for transfers between devices, on_device(): lax.psum_scatter(term.reshape(width * lax.axis_size('tp'), slot_count), '...  89 us
    all_to_all x1, waiting for transfers between devices, on_device(): lax.all_to_all(jnp.stack(jnp.split(summed.astype(jnp.bfloat16), lax.axis_...  27.1 us
    unnamed x45, local copies, waits for them, and re-layouts  23.5 us
    another operation x3, other arithmetic  18.2 us
    dot_general x1, matrix products, on_device(): jnp.einsum('slch,lhd->dslc', hidden, down_proj, preferred_element_type=jn...  14.1 us
    all_gather x1, blocking collectives, on_device(): lax.all_gather(tokens, 'tp', axis=1, tiled=True)  13.7 us
    transpose x1, local copies, waits for them, and re-layouts, on_device(): jnp.einsum('slch,lhd->dslc', hidden, down_proj, preferred_element_type=jn...  11.6 us
  transfers between devices with their start and end apart: 2, of which 2 were waited for; matrix products, arithmetic and copies ran while one was open for 0% of the time, Pallas kernels for 0%

profile of v1, /device:TPU:8, one launch (start us, length us, event | category | flops | bytes accessed | tf_op | source)
XLA Modules:
  0.0 450.1 jit_solution(8107725817888526657)
XLA Ops:
  6.5 0.9 copy.44
  7.6 18.0 %reduce-window.6 = s32[64,8,128]{2,1,0:T(8,128)S(1)} reduce-window(s32[64,8,128]{2,1,0:T(8,128)S(1)} %fusion.39, s32[]{:T(128)} %constant.12.clone.1), window={size=1x1x128 pad=0_0x0_0x127_0}, to_apply=%region_3.4 | reduce-window | flops 8323072 | bytes 524292 | tf_op jit(solution)/shard_map/reduce-window
  26.4 0.7 compare_select_fusion
  27.1 7.4 %fusion = pred[2048,128]{1,0:T(8,128)(4,1)S(1)} fusion(s32[128,8]{0,1:T(8,128)S(1)} %get-tuple-element.6), kind=kLoop, calls=%fused_computation.2 | loop fusion | flops 3932160 | bytes 266240 | tf_op jit(solution)/shard_map/reduce_or | solution.py:29
  34.5 13.7 %all_gather.6 = bf16[128,2048]{1,0:T(8,128)(2,1)S(1)} all-gather(bf16[128,256]{1,0:T(8,128)(2,1)} %param.7), channel_id=1, replica_groups=mesh['ep'=32,'tp'=8] {'tp'}, dimensions={1}, use_global_device_ids=true | all-gather | bytes 589824 | tf_op jit(solution)/shard_map/all_gather | solution.py:31
  48.4 0.7 reshape.103
  49.1 10.2 %all-gather = bf16[8,1,256]{2,1,0:T(2,128)(2,1)S(1)} all-gather(bf16[1,1,256]{2,1,0:T(2,128)(2,1)S(1)} %reshape.103), channel_id=1, replica_groups=mesh['ep'=32,'tp'=8] {'tp'}, dimensions={0}, use_global_device_ids=true | all-gather | bytes 4608 | tf_op jit(solution)/shard_map/all_gather | solution.py:32
  59.3 2.4 convolution_convert_fusion
  61.7 197.5 %all_to_all.14 = bf16[32,64,2048]{2,1,0:T(8,128)(2,1)S(1)} all-to-all(bf16[32,64,2048]{2,1,0:T(8,128)(2,1)S(1)} %bitcast.188), channel_id=1, replica_groups=mesh['ep'=32,'tp'=8] {'ep'}, dimensions={0} | all-to-all | bytes 16777216 | tf_op jit(solution)/shard_map/all_to_all | solution.py:42
  259.2 3.2 copy-done.1
  262.4 2.3 fusion.5
  264.7 14.1 %convolution_bitcast_fusion = f32[2048,32,2,32]{0,3,1,2:T(8,128)} fusion(bf16[32,2,32,2048]{3,2,1,0:T(8,128)(2,1)} %bitcast.190, bf16[2,128,2048]{2,1,0:T(8,128)(2,1)S(1)} %copy-done, bf16[2,2048,128]{2,1,0:T(8,128)(2,1)S(1)} %copy-done.2, f32[32,2,32,128]{3,2,0,1:T(8,128)S(1)} %fusion.5), kind=kOutput, calls=%fused_computation.8 | convolution fusion | flops 2149056512 | bytes 28311552 | tf_op jit(solution)/shard_map/slch,lhd->dslc/dot_general | solution.py:47
  278.9 11.6 %copy.51 = f32[2048,32,2,32]{0,3,2,1:T(8,128)} copy(f32[2048,32,2,32]{0,3,1,2:T(8,128)} %convolution_bitcast_fusion) | data formatting | bytes 33554432 | tf_op jit(solution)/shard_map/slch,lhd->dslc/transpose | solution.py:47
  290.5 89.0 %reduce-scatter.2.cloned.1.call-done = f32[256,2048]{0,1:T(8,128)} async-done(((f32[2048,2048]{0,1:T(8,128)}), f32[256,2048]{0,1:T(8,128)}) %reduce-scatter.2.cloned.1.call-update) | async-done | bytes 2097168 | tf_op jit(solution)/shard_map/reduce_scatter | solution.py:48
  379.5 1.7 convert_element_type.39
  381.8 0.6 constant_dynamic-update-slice_fusion.30
  383.0 0.6 constant_dynamic-update-slice_fusion.28
  384.2 0.6 constant_dynamic-update-slice_fusion.26
  385.4 0.6 constant_dynamic-update-slice_fusion.24
  386.7 0.6 constant_dynamic-update-slice_fusion.22
  387.3 0.6 constant_dynamic-update-slice_fusion.21
  387.9 0.6 constant_dynamic-update-slice_fusion.20
  391.5 0.6 constant_dynamic-update-slice_fusion.14
  392.7 0.6 constant_dynamic-update-slice_fusion.12
  393.9 0.6 constant_dynamic-update-slice_fusion.10
  397.5 0.6 constant_dynamic-update-slice_fusion.4
  399.4 0.6 constant_dynamic-update-slice_fusion.1
  400.0 0.6 constant_dynamic-update-slice_fusion
  400.6 10.2 %all-to-all-start.1 = ((bf16[32,256,64]{1,2,0:T(8,128)(2,1)}), bf16[32,256,64]{1,2,0:T(8,128)(2,1)S(1)}, u32[]{:S(2)}, u32[]{:S(2)}) async-start(bf16[32,256,64]{1,2,0:T(8,128)(2,1)} %constant_dynamic-update-slice_fusion), calls=%async_computation.2 | async-start | bytes 2097152 | tf_op jit(solution)/shard_map/all_to_all | solution.py:52
  411.2 27.1 %all-to-all-done.1 = bf16[32,256,64]{1,2,0:T(8,128)(2,1)S(1)} async-done(((bf16[32,256,64]{1,2,0:T(8,128)(2,1)}), bf16[32,256,64]{1,2,0:T(8,128)(2,1)S(1)}, u32[]{:S(2)}, u32[]{:S(2)}) %all-to-all-start.1) | async-done | bytes 1048608 | tf_op jit(solution)/shard_map/all_to_all | solution.py:52
  438.3 3.9 gather_fusion
  442.2 1.0 fusion.22
  (55 shorter events, 13.0 us)
Async XLA Ops:
  6.5 258.2 %copy-start = (bf16[2,128,2048]{2,1,0:T(8,128)(2,1)S(1)}, bf16[2,128,2048]{2,1,0:T(8,128)(2,1)}, u32[]{:S(2)}) copy-start(bf16[2,128,2048]{2,1,0:T(8,128)(2,1)} %param.13) | copy-start | bytes 3145732
  6.5 373.0 %reduce-scatter.2.cloned.1.call-start = ((), (), s32[]{:S(2)}) async-start(), calls=%async_computation.3 | async-start | bytes 18874368 | tf_op jit(solution)/shard_map/reduce_scatter | solution.py:48
  61.7 200.7 %copy-start.5 = (bf16[2,2048,128]{2,1,0:T(8,128)(2,1)S(1)}, bf16[2,2048,128]{2,1,0:T(8,128)(2,1)}, u32[]{:S(2)}) copy-start(bf16[2,2048,128]{2,1,0:T(8,128)(2,1)} %param.11) | copy-start | bytes 3145732
  259.2 3.2 copy-start.1
  259.2 5.6 %copy-start.2 = (bf16[2,2048,128]{2,1,0:T(8,128)(2,1)S(1)}, bf16[2,2048,128]{2,1,0:T(8,128)(2,1)}, u32[]{:S(2)}) copy-start(bf16[2,2048,128]{2,1,0:T(8,128)(2,1)} %param.12) | copy-start | bytes 3145732
  290.5 120.4 %copy-start.3 = (s32[128,8]{0,1:T(8,128)S(1)}, s32[128,8]{0,1:T(8,128)}, u32[]{:S(2)}) copy-start(s32[128,8]{0,1:T(8,128)} %param.10) | copy-start | bytes 12292
  290.5 120.5 %copy-start.4 = (f32[128,64]{0,1:T(8,128)S(1)}, f32[128,64]{0,1:T(8,128)}, u32[]{:S(2)}) copy-start(f32[128,64]{0,1:T(8,128)} %param.9) | copy-start | bytes 98308
  400.6 37.7 %all-to-all-start.1 = ((bf16[32,256,64]{1,2,0:T(8,128)(2,1)}), bf16[32,256,64]{1,2,0:T(8,128)(2,1)S(1)}, u32[]{:S(2)}, u32[]{:S(2)}) async-start(bf16[32,256,64]{1,2,0:T(8,128)(2,1)} %constant_dynamic-update-slice_fusion), calls=%async_computation.2 | async-start | bytes 2097152 | tf_op jit(solution)/shard_map/all_to_all | solution.py:52
Sparse Core Ops, SparseCore 0:
  290.6 88.8 reduce-scatter.1
